TPU v7x, 32 devices: a whole 2x2x4 slice. The times are simulated.
32 devices in a mesh: dp: 8 (over z, x), row: 2 (over core), col: 2 (over y).
Axes of the slice: x: 2, y: 2, z: 4, core: 2. Of those that a mesh axis runs over, the one named last changes fastest.
Arguments:
- tokens: bfloat16 [2, 8, 256, 2048], P(None, None, 'dp', ('row', 'col')), may hold values from -57 to 57
- lengths: int32 [2, 8], replicated, may hold values from 64 to 256, as said below
- deal_order: int32 [2, 8], replicated, may hold values from 0 to 7, each once within a row
- attention_gain: float32 [2048], P(('row', 'col')), may hold values from 0.25 to 1.75
- query_weight: bfloat16 [2048, 2048], P('row', 'col'), may hold values from -0.1875 to 0.1875
- key_weight: bfloat16 [2048, 2048], P('row', 'col'), may hold values from -0.1875 to 0.1875
- value_weight: bfloat16 [2048, 2048], P('row', 'col'), may hold values from -0.125 to 0.125
- output_weight: bfloat16 [2048, 2048], P('col', 'row'), may hold values from -0.25 to 0.25
- feed_gain: float32 [2048], P(('row', 'col')), may hold values from 0.25 to 1.75
- gate_weight: bfloat16 [2048, 8192], P('row', 'col'), may hold values from -0.125 to 0.125
- up_weight: bfloat16 [2048, 8192], P('row', 'col'), may hold values from -0.125 to 0.125
- down_weight: bfloat16 [8192, 2048], P('col', 'row'), may hold values from -0.09375 to 0.09375
- cotangent: bfloat16 [2, 8, 256, 2048], P(None, 'dp', None, ('row', 'col')), may hold values from -6 to 6
Outputs:
- layer_output: bfloat16 [2, 8, 256, 2048], P(None, None, 'dp', ('row', 'col'))
- tokens_grad: bfloat16 [2, 8, 256, 2048], P(None, None, 'dp', ('row', 'col'))
- attention_gain_grad: float32 [2048], P(('row', 'col', 'dp'))
- query_grad: float32 [2048, 2048], P(('row', 'dp'), 'col')
- key_grad: float32 [2048, 2048], P(('row', 'dp'), 'col')
- value_grad: float32 [2048, 2048], P(('row', 'dp'), 'col')
- output_grad: float32 [2048, 2048], P(('col', 'dp'), 'row')
- feed_gain_grad: float32 [2048], P(('row', 'col', 'dp'))
- gate_grad: float32 [2048, 8192], P(('row', 'dp'), 'col')
- up_grad: float32 [2048, 8192], P(('row', 'dp'), 'col')
- down_grad: float32 [8192, 2048], P(('col', 'dp'), 'row')
Inputs may be any that keep to these rules, and one draw needn't show every extreme that they name: `lengths`: in each micro-batch one sequence has exactly 256 tokens. `deal_order`: each row holds every number of 0 to 7 once.
All inputs are finite; a program needn't handle non-finite values.
Results may differ from a plain program's by a relative error of at most 0.023.
Values may be sent and summed in bfloat16 or wider, within the bound.
A program may use at most 256 MiB of HBM per device.

v0:
```python
import math
import jax
import jax.numpy as jnp
from jax import lax
from jax.sharding import PartitionSpec as P

D = 2048
HEADS = 32
HEAD_DIM = 64
SL = 256
MICRO = 2
EPSILON = 1e-05
ROPE_THETA = 130000.0
MASKED_SCORE = -1000000000.0


def rope_tables(slot_count, head_width):
    half_width = head_width // 2
    frequency = jnp.exp(
        jnp.arange(half_width, dtype=jnp.float32) * (-2.0 * math.log(ROPE_THETA) / head_width)
    )
    angles = jnp.arange(slot_count, dtype=jnp.float32)[:, None] * frequency[None, :]
    return (jnp.cos(angles)[:, None, :], jnp.sin(angles)[:, None, :])


def rotate(values, cosine_table, sine_table):
    half_width = values.shape[-1] // 2
    first_half = values[..., :half_width]
    second_half = values[..., half_width:]
    return jnp.concatenate(
        [
            first_half * cosine_table - second_half * sine_table,
            second_half * cosine_table + first_half * sine_table,
        ],
        axis=-1,
    )


def unrotate(grads, cosine_table, sine_table):
    half_width = grads.shape[-1] // 2
    first_half = grads[..., :half_width]
    second_half = grads[..., half_width:]
    return jnp.concatenate(
        [
            first_half * cosine_table + second_half * sine_table,
            second_half * cosine_table - first_half * sine_table,
        ],
        axis=-1,
    )


def masked_scores(queries, key_rows, length):
    positions = jnp.arange(SL, dtype=jnp.int32)
    allowed = (positions[None, :] <= positions[:, None]) & (positions[None, :] < length)
    scores = jnp.einsum(
        "qhd,khd->hqk", queries, key_rows, preferred_element_type=jnp.float32
    ) * HEAD_DIM ** (-0.5)
    return jnp.where(allowed[None], scores, MASKED_SCORE)


def attend_forward(queries, key_rows, values, length):
    scores = masked_scores(queries, key_rows, length)
    row_top = jnp.max(scores, axis=-1, keepdims=True)
    exp_scores = jnp.exp(scores - row_top)
    row_total = jnp.sum(exp_scores, axis=-1, keepdims=True)
    softmax_out = (exp_scores / row_total).astype(jnp.bfloat16)
    mixed_heads = jnp.einsum(
        "hqk,khd->qhd", softmax_out, values, preferred_element_type=jnp.float32
    )
    return (mixed_heads, row_top + jnp.log(row_total))


def attend_backward(queries, key_rows, values, length, log_total, mixed_grad):
    softmax_out = jnp.exp(masked_scores(queries, key_rows, length) - log_total)
    softmax_grad = jnp.einsum(
        "qhd,khd->hqk", mixed_grad, values, preferred_element_type=jnp.float32
    )
    values_grad = jnp.einsum(
        "hqk,qhd->khd",
        softmax_out.astype(jnp.bfloat16),
        mixed_grad,
        preferred_element_type=jnp.float32,
    )
    row_inner = jnp.sum(softmax_out * softmax_grad, axis=-1, keepdims=True)
    scores_grad = (softmax_out * (softmax_grad - row_inner)).astype(jnp.bfloat16)
    queries_grad = jnp.einsum(
        "hqk,khd->qhd", scores_grad, key_rows, preferred_element_type=jnp.float32
    ) * HEAD_DIM ** (-0.5)
    keys_grad = jnp.einsum(
        "hqk,qhd->khd", scores_grad, queries, preferred_element_type=jnp.float32
    ) * HEAD_DIM ** (-0.5)
    return (queries_grad, keys_grad, values_grad)


def column_gather(values):
    return lax.all_gather(values, "col", axis=1, tiled=True)


def row_scatter(stacked):
    return lax.psum_scatter(stacked, "row", scatter_dimension=2, tiled=True)


def row_gather(stacked):
    return lax.all_gather(stacked, "row", axis=2, tiled=True)


def column_scatter(partial_rows):
    return lax.psum_scatter(
        partial_rows.astype(jnp.bfloat16), "col", scatter_dimension=1, tiled=True
    ).astype(jnp.float32)


def feature_total(row_values):
    return lax.psum(row_values, ("row", "col"))


def norm_scale(values):
    return lax.rsqrt(feature_total(jnp.sum(values * values, axis=1)) / D + EPSILON)


def norm_backward(normed_grad, values, inverse_rms, gain_vector, upstream):
    gain_piece = jnp.sum(normed_grad * values * inverse_rms[:, None], axis=0)
    feature_dot = feature_total(jnp.sum(normed_grad * gain_vector * values, axis=1))
    result = (
        upstream
        + normed_grad * gain_vector * inverse_rms[:, None]
        - values * (inverse_rms**3 * feature_dot / D)[:, None]
    )
    return (result, gain_piece)


def per_device(
    tokens,
    lengths,
    deal_order,
    attention_gain,
    query_weight,
    key_weight,
    value_weight,
    output_weight,
    feed_gain,
    gate_weight,
    up_weight,
    down_weight,
    cotangent,
):
    head_shape = (SL, HEADS // (lax.axis_size("row") * lax.axis_size("col")), HEAD_DIM)
    dealt_rows = lax.all_to_all(
        jnp.take_along_axis(tokens, deal_order[:, :, None, None], axis=1),
        "dp",
        split_axis=1,
        concat_axis=2,
        tiled=True,
    )
    own_order = lax.dynamic_slice_in_dim(deal_order, lax.axis_index("dp"), 1, 1)
    own_lengths = jnp.take_along_axis(lengths, own_order, axis=1)[:, 0]
    cosine_table, sine_table = rope_tables(SL, HEAD_DIM)
    qkv_weights = jnp.stack((query_weight, key_weight, value_weight))
    pair_weights = jnp.stack((gate_weight, up_weight))
    qkv_grad_sum = jnp.zeros(qkv_weights.shape, jnp.float32)
    output_grad_sum = jnp.zeros(output_weight.shape, jnp.float32)
    pair_grad_sum = jnp.zeros(pair_weights.shape, jnp.float32)
    down_grad_sum = jnp.zeros(down_weight.shape, jnp.float32)
    attention_gain_sum = jnp.zeros(attention_gain.shape, jnp.float32)
    feed_gain_sum = jnp.zeros(feed_gain.shape, jnp.float32)
    row_positions = jnp.arange(SL, dtype=jnp.int32)
    output_blocks = []
    grad_blocks = []
    for micro_index in range(MICRO):
        length = own_lengths[micro_index]
        residual_in = dealt_rows[micro_index, 0].astype(jnp.float32)
        upstream = (
            cotangent[micro_index, 0].astype(jnp.float32)
            * (row_positions < length).astype(jnp.float32)[:, None]
        )
        inverse_first = norm_scale(residual_in)
        normed_first = (residual_in * inverse_first[:, None] * attention_gain).astype(jnp.bfloat16)
        normed_first_all = column_gather(normed_first)
        projected = row_scatter(
            jnp.einsum(
                "rd,kde->kre", normed_first_all, qkv_weights, preferred_element_type=jnp.float32
            )
        )
        queries = rotate(projected[0].reshape(head_shape), cosine_table, sine_table).astype(
            jnp.bfloat16
        )
        key_rows = rotate(projected[1].reshape(head_shape), cosine_table, sine_table).astype(
            jnp.bfloat16
        )
        values = projected[2].reshape(head_shape).astype(jnp.bfloat16)
        mixed_heads, log_total = attend_forward(queries, key_rows, values, length)
        mixed_all = row_gather(mixed_heads.reshape(1, SL, -1).astype(jnp.bfloat16))[0]
        middle = residual_in + column_scatter(
            jnp.dot(mixed_all, output_weight, preferred_element_type=jnp.float32)
        )
        inverse_second = norm_scale(middle)
        normed_second = (middle * inverse_second[:, None] * feed_gain).astype(jnp.bfloat16)
        normed_second_all = column_gather(normed_second)
        gate_up = row_scatter(
            jnp.einsum(
                "rd,kde->kre", normed_second_all, pair_weights, preferred_element_type=jnp.float32
            )
        )
        swish_gate = gate_up[0] / (1.0 + jnp.exp(-gate_up[0]))
        hidden = (swish_gate * gate_up[1]).astype(jnp.bfloat16)
        hidden_all = row_gather(hidden[None])[0]
        layer_rows = middle + column_scatter(
            jnp.dot(hidden_all, down_weight, preferred_element_type=jnp.float32)
        )
        output_blocks.append(layer_rows.astype(jnp.bfloat16))
        top_all = column_gather(upstream.astype(jnp.bfloat16))
        down_grad_sum = down_grad_sum + jnp.einsum(
            "rf,rd->fd", hidden_all, top_all, preferred_element_type=jnp.float32
        )
        hidden_grad = row_scatter(
            jnp.einsum("rd,fd->rf", top_all, down_weight, preferred_element_type=jnp.float32)[None]
        )[0]
        sigmoid_gate = 1.0 / (1.0 + jnp.exp(-gate_up[0]))
        gate_grad = (
            hidden_grad * gate_up[1] * sigmoid_gate * (1.0 + gate_up[0] * (1.0 - sigmoid_gate))
        )
        pair_grad_all = row_gather(
            jnp.stack((gate_grad, hidden_grad * swish_gate)).astype(jnp.bfloat16)
        )
        pair_grad_sum = pair_grad_sum + jnp.einsum(
            "rd,kre->kde", normed_second_all, pair_grad_all, preferred_element_type=jnp.float32
        )
        second_grad = column_scatter(
            jnp.einsum(
                "kre,kde->rd", pair_grad_all, pair_weights, preferred_element_type=jnp.float32
            )
        )
        middle_grad, gain_piece = norm_backward(
            second_grad, middle, inverse_second, feed_gain, upstream
        )
        feed_gain_sum = feed_gain_sum + gain_piece
        branch_all = column_gather(middle_grad.astype(jnp.bfloat16))
        output_grad_sum = output_grad_sum + jnp.einsum(
            "rh,rd->hd", mixed_all, branch_all, preferred_element_type=jnp.float32
        )
        mixed_grad = row_scatter(
            jnp.einsum("rd,hd->rh", branch_all, output_weight, preferred_element_type=jnp.float32)[
                None
            ]
        )[0]
        queries_grad, keys_grad, values_grad = attend_backward(
            queries,
            key_rows,
            values,
            length,
            log_total,
            mixed_grad.reshape(head_shape).astype(jnp.bfloat16),
        )
        turned_back = jnp.stack(
            (
                unrotate(queries_grad, cosine_table, sine_table),
                unrotate(keys_grad, cosine_table, sine_table),
                values_grad,
            )
        )
        three_all = row_gather(turned_back.reshape(3, SL, -1).astype(jnp.bfloat16))
        qkv_grad_sum = qkv_grad_sum + jnp.einsum(
            "rd,kre->kde", normed_first_all, three_all, preferred_element_type=jnp.float32
        )
        first_grad = column_scatter(
            jnp.einsum("kre,kde->rd", three_all, qkv_weights, preferred_element_type=jnp.float32)
        )
        input_grad, gain_piece = norm_backward(
            first_grad, residual_in, inverse_first, attention_gain, middle_grad
        )
        attention_gain_sum = attention_gain_sum + gain_piece
        grad_blocks.append(input_grad.astype(jnp.bfloat16))
    reduced = (
        lax.psum_scatter(
            attention_gain_sum.astype(jnp.bfloat16), "dp", scatter_dimension=0, tiled=True
        ).astype(jnp.float32),
        lax.psum_scatter(
            qkv_grad_sum[0].astype(jnp.bfloat16), "dp", scatter_dimension=0, tiled=True
        ).astype(jnp.float32),
        lax.psum_scatter(
            qkv_grad_sum[1].astype(jnp.bfloat16), "dp", scatter_dimension=0, tiled=True
        ).astype(jnp.float32),
        lax.psum_scatter(
            qkv_grad_sum[2].astype(jnp.bfloat16), "dp", scatter_dimension=0, tiled=True
        ).astype(jnp.float32),
        lax.psum_scatter(
            output_grad_sum.astype(jnp.bfloat16), "dp", scatter_dimension=0, tiled=True
        ).astype(jnp.float32),
        lax.psum_scatter(
            feed_gain_sum.astype(jnp.bfloat16), "dp", scatter_dimension=0, tiled=True
        ).astype(jnp.float32),
        lax.psum_scatter(
            pair_grad_sum[0].astype(jnp.bfloat16), "dp", scatter_dimension=0, tiled=True
        ).astype(jnp.float32),
        lax.psum_scatter(
            pair_grad_sum[1].astype(jnp.bfloat16), "dp", scatter_dimension=0, tiled=True
        ).astype(jnp.float32),
        lax.psum_scatter(
            down_grad_sum.astype(jnp.bfloat16), "dp", scatter_dimension=0, tiled=True
        ).astype(jnp.float32),
    )
    returned_out, returned_grad = (
        lax.all_to_all(
            jnp.stack(output_blocks)[:, None], "dp", split_axis=2, concat_axis=1, tiled=True
        ),
        lax.all_to_all(
            jnp.stack(grad_blocks)[:, None], "dp", split_axis=2, concat_axis=1, tiled=True
        ),
    )
    slot_of = jnp.argsort(deal_order, axis=1)[:, :, None, None]
    layer_output = jnp.take_along_axis(returned_out, slot_of, axis=1)
    tokens_grad = jnp.take_along_axis(returned_grad, slot_of, axis=1)
    return (
        layer_output,
        tokens_grad,
        reduced[0],
        reduced[1],
        reduced[2],
        reduced[3],
        reduced[4],
        reduced[5],
        reduced[6],
        reduced[7],
        reduced[8],
    )


def solution(mesh):
    in_specs = (
        P(None, None, "dp", ("row", "col")),
        P(),
        P(),
        P(("row", "col")),
        P("row", "col"),
        P("row", "col"),
        P("row", "col"),
        P("col", "row"),
        P(("row", "col")),
        P("row", "col"),
        P("row", "col"),
        P("col", "row"),
        P(None, "dp", None, ("row", "col")),
    )
    out_specs = (
        P(None, None, "dp", ("row", "col")),
        P(None, None, "dp", ("row", "col")),
        P(("row", "col", "dp")),
        P(("row", "dp"), "col"),
        P(("row", "dp"), "col"),
        P(("row", "dp"), "col"),
        P(("col", "dp"), "row"),
        P(("row", "col", "dp")),
        P(("row", "dp"), "col"),
        P(("row", "dp"), "col"),
        P(("col", "dp"), "row"),
    )
    return jax.shard_map(
        per_device, mesh=mesh, in_specs=in_specs, out_specs=out_specs, check_vma=False
    )
```

profile of v0, /device:TPU:0, one launch (start us, length us, event | category | flops | bytes accessed | tf_op | source)
XLA Modules:
  0.0 1240.4 jit_solution(1370745527233818062)
XLA Ops:
  11.4 7.3 all-to-all-start
  18.7 3.9 copy.152
  22.6 3.9 copy.153
  26.6 3.9 copy.154
  33.5 7.5 all-reduce.5
  41.7 9.3 all_gather.52
  51.8 6.3 convolution_bitcast_fusion.4
  58.2 8.5 all_gather.48
  67.5 6.4 convolution_bitcast_fusion.5
  102.4 10.7 all_gather.60
  113.9 7.9 convolution_bitcast_fusion.2
  121.8 12.0 copy.158
  133.8 12.3 copy.159
  147.9 7.0 all-reduce.4
  158.1 8.9 all_gather.54
  167.8 10.3 convolution_bitcast_fusion
  178.1 7.8 all_gather.56
  186.7 9.7 convolution_bitcast_fusion.3
  197.4 7.0 all_gather.50
  205.2 11.7 convolution_bitcast_fusion.1
  217.5 4.9 multiply_convert_fusion.2
  224.1 10.2 reduce-scatter.38.cloned.1.call-done
  234.3 4.9 multiply_convert_fusion.5
  241.6 9.2 all-gather.15.cloned.1.call-done
  250.8 10.1 fusion.24
  261.0 6.1 all-gather.11.cloned.1.call-done
  267.1 10.1 fusion.23
  277.3 3.1 all-gather.9.cloned.1.call-done
  280.4 7.2 fusion.20
  287.7 11.2 reduce-scatter.60.cloned.1.call-done
  298.9 17.5 %reduce-scatter.52.cloned.1.call-done = bf16[256,512]{1,0:T(8,128)(2,1)} async-done(((bf16[256,1024]{1,0:T(8,128)(2,1)}), bf16[256,512]{1,0:T(8,128)(2,1)}) %reduce-scatter.52.cloned.1.call-update) | async-done | bytes 262160 | tf_op jit(solution)/shard_map/reduce_scatter | solution.py:108
  318.6 7.0 all-reduce.3
  328.0 5.5 reduce-scatter.48.cloned.1.call-done
  336.2 8.7 all_gather.58
  347.5 8.1 all_gather.62
  380.5 2.7 add_convert_fusion.9
  403.6 5.3 fusion.15
  409.0 4.8 all-gather.17.cloned.1.call-done
  413.8 5.3 fusion.16
  419.1 8.0 all-gather.7.cloned.1.call-done
  427.2 7.2 fusion.17
  438.7 3.4 fusion.80
  444.0 2.7 slice_bitcast_fusion.2
  446.8 3.9 copy.216
  450.8 3.9 copy.214
  458.9 9.3 fusion.5
  468.3 11.7 add_convert_fusion.1
  481.0 15.7 %fusion.74 = f32[2,4096,1024]{2,1,0:T(8,128)} fusion(bf16[2,256,4096]{1,2,0:T(8,128)(2,1)} %all-gather.11.cloned.1.call-done, bf16[256,1024]{1,0:T(8,128)(2,1)S(1)} %copy-done.32), kind=kOutput, calls=%fused_computation.147 | convolution fusion | flops 4294967296 | bytes 38273024 | tf_op jit(solution)/shard_map/rd,kre->kde/dot_general | solution.py:225
  496.8 19.1 %fusion = bf16[2,1024,4096]{1,2,0:T(8,128)(2,1)} fusion(f32[2,4096,1024]{2,1,0:T(8,128)} %fusion.74, bf16[2,256,4096]{1,2,0:T(8,128)(2,1)S(1)} %copy-done.23, bf16[256,1024]{1,0:T(8,128)(2,1)S(1)} %copy-done.30), kind=kOutput, calls=%fused_computation.5 | convolution fusion | flops 4311744512 | bytes 55050240 | tf_op jit(solution)/shard_map/rd,kre->kde/dot_general | solution.py:225
  515.9 11.7 slice_bitcast_fusion
  527.7 11.3 copy.220
  539.0 11.6 copy.218
  552.9 7.7 all-reduce.2
  563.7 5.9 all-to-all-start.1
  572.2 21.8 %all-to-all-done.1 = bf16[2,1,256,512]{3,0,1,2:T(2,128)(2,1)S(1)} async-done(((bf16[2,1,256,512]{3,0,1,2:T(2,128)(2,1)}), bf16[2,1,256,512]{3,0,1,2:T(2,128)(2,1)S(1)}, u32[]{:S(2)}, u32[]{:S(2)}) %all-to-all-start.1) | async-done | bytes 524320 | tf_op jit(solution)/shard_map/all_to_all | solution.py:303
  594.0 3.9 all-to-all-start.2
  601.1 22.1 %all-reduce.6 = (bf16[512]{0:T(512)(128)(2,1)S(1)}, bf16[512]{0:T(512)(128)(2,1)S(1)}) all-reduce(bf16[512]{0:T(512)(128)(2,1)S(1)} %add_convert_fusion.15, bf16[512]{0:T(512)(128)(2,1)S(1)} %add_convert_fusion.14), channel_id=18, replica_groups=mesh['dp'=8,'row'=2,'col'=2] {'dp'}, use_global_device_ids=true, to_apply=%region_41.43.clone | all-reduce | flops 1024 | bytes 4096
  626.9 6.0 reduce-scatter.74.cloned.1.call-done
  635.0 68.9 %reduce-scatter.72.cloned.1.call-done = bf16[128,1024]{1,0:T(8,128)(2,1)} async-done(((bf16[1024,1024]{1,0:T(8,128)(2,1)}), bf16[128,1024]{1,0:T(8,128)(2,1)}) %reduce-scatter.72.cloned.1.call-update) | async-done | bytes 262160
  705.9 68.8 %reduce-scatter.70.cloned.1.call-done = bf16[128,1024]{1,0:T(8,128)(2,1)} async-done(((bf16[1024,1024]{1,0:T(8,128)(2,1)}), bf16[128,1024]{1,0:T(8,128)(2,1)}) %reduce-scatter.70.cloned.1.call-update) | async-done | bytes 262160
  776.7 149.5 %reduce-scatter.68.cloned.1.call-done = bf16[512,1024]{1,0:T(8,128)(2,1)} async-done(((bf16[4096,1024]{1,0:T(8,128)(2,1)}), bf16[512,1024]{1,0:T(8,128)(2,1)}) %reduce-scatter.68.cloned.1.call-update) | async-done | bytes 1048592 | tf_op jit(solution)/shard_map/reduce_scatter | solution.py:298
  926.2 2.8 convert_element_type.355
  929.0 149.4 %reduce-scatter.78.cloned.1.call-done = bf16[128,4096]{1,0:T(8,128)(2,1)} async-done(((bf16[1024,4096]{1,0:T(8,128)(2,1)}), bf16[128,4096]{1,0:T(8,128)(2,1)}) %reduce-scatter.78.cloned.1.call-update) | async-done | bytes 1048592
  1081.6 148.4 %reduce-scatter.76.cloned.1.call-done = bf16[128,4096]{1,0:T(8,128)(2,1)} async-done(((bf16[1024,4096]{1,0:T(8,128)(2,1)}), bf16[128,4096]{1,0:T(8,128)(2,1)}) %reduce-scatter.76.cloned.1.call-update) | async-done | bytes 1048592
  (370 shorter events, 145.2 us)
Async XLA Ops:
  7.2 84.0 %copy-start = (bf16[1024,1024]{1,0:T(8,128)(2,1)S(1)}, bf16[1024,1024]{1,0:T(8,128)(2,1)}, u32[]{:S(2)}) copy-start(bf16[1024,1024]{1,0:T(8,128)(2,1)} %param.22) | copy-start | bytes 6291460
  11.4 21.7 %all-to-all-start = ((bf16[2,8,32,512]{3,2,0,1:T(8,128)(2,1)}), bf16[2,8,32,512]{3,2,0,1:T(8,128)(2,1)S(1)}, u32[]{:S(2)}, u32[]{:S(2)}) async-start(bf16[2,8,32,512]{3,2,0,1:T(8,128)(2,1)} %copy.151), calls=%async_computation | async-start | bytes 1048576 | tf_op jit(solution)/shard_map/all_to_all | solution.py:148
  18.6 62.7 %reduce-scatter.42.cloned.1.call-start = ((), (), s32[]{:S(2)}) async-start(), calls=%async_computation.31 | async-start | bytes 4718592 | tf_op jit(solution)/shard_map/reduce_scatter | solution.py:100
  26.6 15.0 %copy-start.63 = (f32[512]{0:T(512)S(1)}, f32[512]{0:T(512)}, u32[]{:S(2)}) copy-start(f32[512]{0:T(512)} %param.18) | copy-start | bytes 6148
  41.0 10.1 copy-start.73
  41.0 10.1 copy-start.75
  58.2 25.3 %reduce-scatter.34.cloned.1.call-start = ((), (), s32[]{:S(2)}) async-start(), calls=%async_computation.26 | async-start | bytes 4718592 | tf_op jit(solution)/shard_map/reduce_scatter | solution.py:100
  73.9 72.2 %reduce-scatter.36.cloned.1.call-start = ((), (), s32[]{:S(2)}) async-start(), calls=%async_computation.27 | async-start | bytes 786432 | tf_op jit(solution)/shard_map/reduce_scatter | solution.py:108
  79.0 22.1 %copy-start.69 = (f32[256]{0:T(256)}, f32[256]{0:T(256)S(1)}, u32[]{:S(2)}) copy-start(f32[256]{0:T(256)S(1)} %get-tuple-element.152) | copy-start | bytes 3076
  79.0 22.1 %copy-start.71 = (f32[256]{0:T(256)}, f32[256]{0:T(256)S(1)}, u32[]{:S(2)}) copy-start(f32[256]{0:T(256)S(1)} %get-tuple-element.153) | copy-start | bytes 3076
  85.9 6.9 copy-start.42
  92.7 53.4 %reduce-scatter.44.cloned.1.call-start = ((), (), s32[]{:S(2)}) async-start(), calls=%async_computation.32 | async-start | bytes 786432 | tf_op jit(solution)/shard_map/reduce_scatter | solution.py:108
  101.1 116.4 %reduce-scatter.58.cloned.1.call-start = ((), (), s32[]{:S(2)}) async-start(), calls=%async_computation.42 | async-start | bytes 6291456 | tf_op jit(solution)/shard_map/reduce_scatter | solution.py:100
  121.8 95.7 %reduce-scatter.46.cloned.1.call-start = ((), (), s32[]{:S(2)}) async-start(), calls=%async_computation.33 | async-start | bytes 12582912 | tf_op jit(solution)/shard_map/reduce_scatter | solution.py:100
  133.8 22.4 %copy-start.59 = (f32[512]{0:T(512)S(1)}, f32[512]{0:T(512)}, u32[]{:S(2)}) copy-start(f32[512]{0:T(512)} %param.23) | copy-start | bytes 6148
  156.2 10.8 copy-start.65
  178.1 46.0 %reduce-scatter.50.cloned.1.call-start = ((), (), s32[]{:S(2)}) async-start(), calls=%async_computation.36 | async-start | bytes 6291456 | tf_op jit(solution)/shard_map/reduce_scatter | solution.py:100
  196.5 37.8 %reduce-scatter.38.cloned.1.call-start = ((), (), s32[]{:S(2)}) async-start(), calls=%async_computation.28 | async-start | bytes 12582912 | tf_op jit(solution)/shard_map/reduce_scatter | solution.py:100
  217.0 33.8 %all-gather.15.cloned.1.call-start = ((), (), s32[]{:S(2)}) async-start(), calls=%async_computation.43 | async-start | bytes 6291456 | tf_op jit(solution)/shard_map/all_gather | solution.py:104
  224.0 43.1 %all-gather.11.cloned.1.call-start = ((), (), s32[]{:S(2)}) async-start(), calls=%async_computation.37 | async-start | bytes 6291456 | tf_op jit(solution)/shard_map/all_gather | solution.py:104
  240.8 39.6 %all-gather.9.cloned.1.call-start = ((), (), s32[]{:S(2)}) async-start(), calls=%async_computation.34 | async-start | bytes 3145728 | tf_op jit(solution)/shard_map/all_gather | solution.py:104
  241.5 57.3 %reduce-scatter.60.cloned.1.call-start = ((), (), s32[]{:S(2)}) async-start(), calls=%async_computation.44 | async-start | bytes 786432 | tf_op jit(solution)/shard_map/reduce_scatter | solution.py:108
  261.0 55.4 %reduce-scatter.52.cloned.1.call-start = ((), (), s32[]{:S(2)}) async-start(), calls=%async_computation.38 | async-start | bytes 786432 | tf_op jit(solution)/shard_map/reduce_scatter | solution.py:108
  277.2 39.1 %copy-start.10 = (bf16[256,512]{1,0:T(8,128)(2,1)S(1)}, bf16[256,512]{1,0:T(8,128)(2,1)}, u32[]{:S(2)}) copy-start(bf16[256,512]{1,0:T(8,128)(2,1)} %reduce-scatter.44.cloned.1.call-done) | copy-start | bytes 786436
  277.2 56.3 %reduce-scatter.48.cloned.1.call-start = ((), (), s32[]{:S(2)}) async-start(), calls=%async_computation.35 | async-start | bytes 786432 | tf_op jit(solution)/shard_map/reduce_scatter | solution.py:108
  287.6 72.9 %reduce-scatter.54.cloned.1.call-start = ((), (), s32[]{:S(2)}) async-start(), calls=%async_computation.39 | async-start | bytes 1572864 | tf_op jit(solution)/shard_map/reduce_scatter | solution.py:100
  347.4 22.8 %reduce-scatter.62.cloned.1.call-start = ((), (), s32[]{:S(2)}) async-start(), calls=%async_computation.45 | async-start | bytes 1572864 | tf_op jit(solution)/shard_map/reduce_scatter | solution.py:100
  358.1 45.5 %all-gather.13.cloned.1.call-start = ((), (), s32[]{:S(2)}) async-start(), calls=%async_computation.40 | async-start | bytes 2359296 | tf_op jit(solution)/shard_map/all_gather | solution.py:104
  391.3 22.5 %all-gather.17.cloned.1.call-start = ((), (), s32[]{:S(2)}) async-start(), calls=%async_computation.46 | async-start | bytes 2359296 | tf_op jit(solution)/shard_map/all_gather | solution.py:104
  402.8 24.4 %all-gather.7.cloned.1.call-start = ((), (), s32[]{:S(2)}) async-start(), calls=%async_computation.29 | async-start | bytes 3145728 | tf_op jit(solution)/shard_map/all_gather | solution.py:104
  403.6 147.2 %reduce-scatter.56.cloned.1.call-start = ((), (), s32[]{:S(2)}) async-start(), calls=%async_computation.41 | async-start | bytes 786432 | tf_op jit(solution)/shard_map/reduce_scatter | solution.py:108
  408.9 141.8 %reduce-scatter.64.cloned.1.call-start = ((), (), s32[]{:S(2)}) async-start(), calls=%async_computation.47 | async-start | bytes 786432 | tf_op jit(solution)/shard_map/reduce_scatter | solution.py:108
  419.1 15.6 %copy-start.21 = (bf16[256,1024]{1,0:T(8,128)(2,1)S(1)}, bf16[256,1024]{1,0:T(8,128)(2,1)}, u32[]{:S(2)}) copy-start(bf16[256,1024]{1,0:T(8,128)(2,1)} %copy-done.20) | copy-start | bytes 1572868
  419.1 141.5 %reduce-scatter.40.cloned.1.call-start = ((), (), s32[]{:S(2)}) async-start(), calls=%async_computation.30 | async-start | bytes 786432 | tf_op jit(solution)/shard_map/reduce_scatter | solution.py:108
  434.4 164.9 %reduce-scatter.66.cloned.1.call-start = ((), (), s32[]{:S(2)}) async-start(), calls=%async_computation.48 | async-start | bytes 2359296 | tf_op jit(solution)/shard_map/reduce_scatter | solution.py:286
  437.7 195.2 %reduce-scatter.74.cloned.1.call-start = ((), (), s32[]{:S(2)}) async-start(), calls=%async_computation.52 | async-start | bytes 2359296
  450.7 253.1 %reduce-scatter.72.cloned.1.call-start = ((), (), s32[]{:S(2)}) async-start(), calls=%async_computation.51 | async-start | bytes 2359296
  454.7 319.9 %reduce-scatter.70.cloned.1.call-start = ((), (), s32[]{:S(2)}) async-start(), calls=%async_computation.50 | async-start | bytes 2359296
  457.4 10.9 copy-start.18
  457.4 468.8 %reduce-scatter.68.cloned.1.call-start = ((), (), s32[]{:S(2)}) async-start(), calls=%async_computation.49 | async-start | bytes 9437184 | tf_op jit(solution)/shard_map/reduce_scatter | solution.py:298
  458.9 9.3 copy-start.9
  480.0 16.8 %copy-start.30 = (bf16[256,1024]{1,0:T(8,128)(2,1)S(1)}, bf16[256,1024]{1,0:T(8,128)(2,1)}, u32[]{:S(2)}) copy-start(bf16[256,1024]{1,0:T(8,128)(2,1)} %copy-done.29) | copy-start | bytes 1572868
  480.0 598.4 %reduce-scatter.78.cloned.1.call-start = ((), (), s32[]{:S(2)}) async-start(), calls=%async_computation.54 | async-start | bytes 9437184
  481.0 15.7 %copy-start.23 = (bf16[2,256,4096]{1,2,0:T(8,128)(2,1)S(1)}, bf16[2,256,4096]{1,2,0:T(8,128)(2,1)}, u32[]{:S(2)}) copy-start(bf16[2,256,4096]{1,2,0:T(8,128)(2,1)} %all-gather.15.cloned.1.call-done) | copy-start | bytes 12582916
  539.0 691.1 %reduce-scatter.76.cloned.1.call-start = ((), (), s32[]{:S(2)}) async-start(), calls=%async_computation.53 | async-start | bytes 9437184
  550.6 10.0 copy-start.84
  550.6 10.0 copy-start.11
  550.6 10.0 copy-start.22
  550.6 10.0 copy-start.26
  550.6 10.0 copy-start.70
  550.6 10.0 copy-start.77
  550.7 11.6 copy-start.39
  562.2 7.3 copy-start.68
  562.2 8.1 copy-start.82
  562.2 8.1 copy-start.25
  562.3 8.1 copy-start.41
  562.3 8.1 copy-start.66
  562.3 8.1 copy-start.72
  562.3 8.1 copy-start.78
  563.7 30.3 %all-to-all-start.1 = ((bf16[2,1,256,512]{3,0,1,2:T(2,128)(2,1)}), bf16[2,1,256,512]{3,0,1,2:T(2,128)(2,1)S(1)}, u32[]{:S(2)}, u32[]{:S(2)}) async-start(bf16[2,1,256,512]{3,0,1,2:T(2,128)(2,1)} %copy.161), calls=%async_computation.9 | async-start | bytes 1048576 | tf_op jit(solution)/shard_map/all_to_all | solution.py:303
  570.4 27.6 %copy-start.85 = (u32[32]{0:T(128)S(1)}, u32[32]{0:T(128)}, u32[]{:S(2)}) copy-start(u32[32]{0:T(128)} %constant.126) | copy-start | bytes 388
  570.5 28.8 %copy-start.79 = (f32[512]{0:T(512)S(1)}, f32[512]{0:T(512)}, u32[]{:S(2)}) copy-start(f32[512]{0:T(512)} %get-tuple-element.60) | copy-start | bytes 6148
  570.5 28.8 %copy-start.80 = (f32[512]{0:T(512)S(1)}, f32[512]{0:T(512)}, u32[]{:S(2)}) copy-start(f32[512]{0:T(512)} %get-tuple-element.69) | copy-start | bytes 6148
  594.0 31.0 %all-to-all-start.2 = ((bf16[2,1,256,512]{3,0,1,2:T(2,128)(2,1)}), bf16[2,1,256,512]{3,0,1,2:T(2,128)(2,1)S(1)}, u32[]{:S(2)}, u32[]{:S(2)}) async-start(bf16[2,1,256,512]{3,0,1,2:T(2,128)(2,1)} %copy.185), calls=%async_computation.18 | async-start | bytes 1048576 | tf_op jit(solution)/shard_map/all_to_all | solution.py:306
  (54 other events, 89.3 us)
Sparse Core Ops, SparseCore 0:
  58.3 9.0 reduce-scatter.41
  74.0 9.3 reduce-scatter.33
  92.8 16.9 reduce-scatter.35
  112.6 14.3 reduce-scatter.43
  129.1 12.0 reduce-scatter.57
  178.2 17.2 reduce-scatter.45
  197.9 13.2 reduce-scatter.49
  217.1 17.1 reduce-scatter.37
  235.8 14.9 all-gather.14
  252.2 14.8 all-gather.10
  268.6 11.7 all-gather.8
  283.1 15.7 reduce-scatter.59
  301.8 14.5 reduce-scatter.51
  319.0 14.5 reduce-scatter.47
  347.5 8.5 reduce-scatter.53
  358.2 9.6 reduce-scatter.61
  391.4 9.8 all-gather.12
  402.9 10.8 all-gather.16
  415.4 11.7 all-gather.6
  429.9 15.7 reduce-scatter.55
  448.5 14.5 reduce-scatter.63
  466.0 14.5 reduce-scatter.39
  484.1 67.7 reduce-scatter.65
  555.3 77.5 reduce-scatter.73
  637.0 66.7 reduce-scatter.71
  707.8 66.8 reduce-scatter.69
  778.2 148.0 reduce-scatter.67
  930.3 148.0 reduce-scatter.77
  1082.0 147.9 reduce-scatter.75
where the time goes:
time: 1250 us; the launch traced here: 1240 us
  waiting for transfers between devices  693 us (55%)
  matrix products  182 us (15%)
  local copies, waits for them, and re-layouts  140 us (11%)
  blocking collectives  125 us (10%)
  other arithmetic  65.1 us (5%)
  starting transfers between devices  19.2 us (2%)
  between operations  16.4 us (1%)
    unnamed x34, waiting for transfers between devices  443 us
    reduce_scatter x1, waiting for transfers between devices, per_device(): lax.psum_scatter(down_grad_sum.astype(jnp.bfloat16), 'dp', scatter_dimens...  149 us
    unnamed x195, local copies, waits for them, and re-layouts  97.5 us
    all_gather x8, blocking collectives, column_gather(): return lax.all_gather(values, 'col', axis=1, tiled=True)  69 us
    dot_general x2, matrix products, per_device(): jnp.einsum('rd,kre->kde', normed_second_all, pair_grad_all, preferred_ele...  34.9 us
    reduce_scatter x8, waiting for transfers between devices, column_scatter(): lax.psum_scatter(partial_rows.astype(jnp.bfloat16), 'col', scatter_dimens...  34.2 us
    all_gather x6, waiting for transfers between devices, row_gather(): return lax.all_gather(stacked, 'row', axis=2, tiled=True)  31.3 us
    psum x4, blocking collectives, feature_total(): return lax.psum(row_values, ('row', 'col'))  29.1 us
  transfers between devices with their start and end apart: 32, of which 17 were waited for; matrix products, arithmetic and copies ran while one was open for 26% of the time, Pallas kernels for 0%

commit v1 on v0

--- a/solution.py
+++ b/solution.py
@@ -111,7 +111,7 @@
 
 
 def feature_total(row_values):
-    return lax.psum(row_values, ("row", "col"))
+    return lax.psum(lax.psum(row_values, "row"), "col")
 
 
 def norm_scale(values):

time: 1250 us -> 1250 us (level)
    psum x4 -> x8, blocking collectives: 29.1 us -> 32.4 us  [feature_total(): return lax.psum(lax.psum(row_values, 'row'), 'col')]
  transfers between devices with their start and end apart: 32 -> 32, of which waited for: 17 -> 18; matrix products, arithmetic and copies ran while one was open for 26% -> 26% of each run, Pallas kernels for 0% -> 0%
where the time goes in v1:
time: 1250 us; the launch traced here: 1240 us
  waiting for transfers between devices  692 us (55%)
  matrix products  182 us (15%)
  local copies, waits for them, and re-layouts  140 us (11%)
  blocking collectives  123 us (10%)
  other arithmetic  65.1 us (5%)
  starting transfers between devices  19 us (2%)
  between operations  16.3 us (1%)
    unnamed x34, waiting for transfers between devices  444 us
    reduce_scatter x1, waiting for transfers between devices, per_device(): lax.psum_scatter(down_grad_sum.astype(jnp.bfloat16), 'dp', scatter_dimens...  149 us
    unnamed x195, local copies, waits for them, and re-layouts  97.8 us
    all_gather x8, blocking collectives, column_gather(): return lax.all_gather(values, 'col', axis=1, tiled=True)  64.5 us
    dot_general x2, matrix products, per_device(): jnp.einsum('rd,kre->kde', normed_second_all, pair_grad_all, preferred_ele...  34.9 us
    reduce_scatter x8, waiting for transfers between devices, column_scatter(): lax.psum_scatter(partial_rows.astype(jnp.bfloat16), 'col', scatter_dimens...  32.5 us
    psum x8, blocking collectives, feature_total(): return lax.psum(lax.psum(row_values, 'row'), 'col')  32.4 us
    all_gather x6, waiting for transfers between devices, row_gather(): return lax.all_gather(stacked, 'row', axis=2, tiled=True)  31.2 us
  transfers between devices with their start and end apart: 32, of which 18 were waited for; matrix products, arithmetic and copies ran while one was open for 26% of the time, Pallas kernels for 0%

profile of v1, /device:TPU:0, one launch (start us, length us, event | category | flops | bytes accessed | tf_op | source)
XLA Modules:
  0.0 1238.1 jit_solution(9086319141018543188)
XLA Ops:
  11.4 7.3 all-to-all-start
  18.7 3.9 copy.152
  22.6 3.9 copy.153
  26.6 3.9 copy.154
  35.9 4.9 all-reduce.5
  41.6 7.9 all_gather.52
  50.3 6.3 convolution_bitcast_fusion.4
  56.7 7.0 all_gather.48
  64.5 6.7 convolution_bitcast_fusion.5
  100.3 10.8 all_gather.60
  111.8 7.8 convolution_bitcast_fusion.2
  119.7 12.0 copy.158
  131.7 12.3 copy.159
  145.9 3.1 all-reduce.8
  149.0 5.6 all-reduce.4
  157.8 7.9 all_gather.54
  166.5 10.2 convolution_bitcast_fusion
  176.8 7.0 all_gather.56
  184.7 9.7 convolution_bitcast_fusion.3
  195.3 7.0 all_gather.50
  203.1 11.7 convolution_bitcast_fusion.1
  215.4 4.9 multiply_convert_fusion.2
  221.9 10.0 reduce-scatter.38.cloned.1.call-done
  232.0 4.9 multiply_convert_fusion.5
  239.2 9.2 all-gather.15.cloned.1.call-done
  248.5 10.1 fusion.24
  258.6 6.1 all-gather.11.cloned.1.call-done
  264.7 10.1 fusion.23
  274.9 3.1 all-gather.9.cloned.1.call-done
  278.1 7.2 fusion.20
  285.3 11.2 reduce-scatter.60.cloned.1.call-done
  296.5 17.5 %reduce-scatter.52.cloned.1.call-done = bf16[256,512]{1,0:T(8,128)(2,1)} async-done(((bf16[256,1024]{1,0:T(8,128)(2,1)}), bf16[256,512]{1,0:T(8,128)(2,1)}) %reduce-scatter.52.cloned.1.call-update) | async-done | bytes 262160 | tf_op jit(solution)/shard_map/reduce_scatter | solution.py:108
  316.2 3.1 all-reduce.7
  319.3 5.6 all-reduce.3
  327.4 3.8 reduce-scatter.48.cloned.1.call-done
  333.8 8.7 all_gather.58
  345.1 8.1 all_gather.62
  401.3 5.3 fusion.15
  406.7 4.7 all-gather.17.cloned.1.call-done
  411.4 5.3 fusion.16
  416.7 8.0 all-gather.7.cloned.1.call-done
  424.8 7.2 fusion.17
  436.3 3.4 fusion.80
  444.4 3.9 copy.216
  448.4 3.9 copy.214
  456.5 9.3 fusion.5
  465.8 11.7 add_convert_fusion.1
  478.6 15.7 %fusion.74 = f32[2,4096,1024]{2,1,0:T(8,128)} fusion(bf16[2,256,4096]{1,2,0:T(8,128)(2,1)} %all-gather.11.cloned.1.call-done, bf16[256,1024]{1,0:T(8,128)(2,1)S(1)} %copy-done.32), kind=kOutput, calls=%fused_computation.147 | convolution fusion | flops 4294967296 | bytes 38273024 | tf_op jit(solution)/shard_map/rd,kre->kde/dot_general | solution.py:225
  494.3 19.1 %fusion = bf16[2,1024,4096]{1,2,0:T(8,128)(2,1)} fusion(f32[2,4096,1024]{2,1,0:T(8,128)} %fusion.74, bf16[2,256,4096]{1,2,0:T(8,128)(2,1)S(1)} %copy-done.23, bf16[256,1024]{1,0:T(8,128)(2,1)S(1)} %copy-done.30), kind=kOutput, calls=%fused_computation.5 | convolution fusion | flops 4311744512 | bytes 55050240 | tf_op jit(solution)/shard_map/rd,kre->kde/dot_general | solution.py:225
  513.5 11.8 slice_bitcast_fusion
  525.2 11.3 copy.220
  536.6 11.8 copy.218
  553.3 4.9 all-reduce.2
  561.3 5.9 all-to-all-start.1
  569.9 21.5 %all-to-all-done.1 = bf16[2,1,256,512]{3,0,1,2:T(2,128)(2,1)S(1)} async-done(((bf16[2,1,256,512]{3,0,1,2:T(2,128)(2,1)}), bf16[2,1,256,512]{3,0,1,2:T(2,128)(2,1)S(1)}, u32[]{:S(2)}, u32[]{:S(2)}) %all-to-all-start.1) | async-done | bytes 524320 | tf_op jit(solution)/shard_map/all_to_all | solution.py:303
  591.4 3.6 all-to-all-start.2
  598.2 22.2 %all-reduce.10 = (bf16[512]{0:T(512)(128)(2,1)S(1)}, bf16[512]{0:T(512)(128)(2,1)S(1)}) all-reduce(bf16[512]{0:T(512)(128)(2,1)S(1)} %add_convert_fusion.15, bf16[512]{0:T(512)(128)(2,1)S(1)} %add_convert_fusion.14), channel_id=18, replica_groups=mesh['dp'=8,'row'=2,'col'=2] {'dp'}, use_global_device_ids=true, to_apply=%region_49.51.clone | all-reduce | flops 1024 | bytes 4096
  624.0 6.5 reduce-scatter.74.cloned.1.call-done
  632.6 68.9 %reduce-scatter.72.cloned.1.call-done = bf16[128,1024]{1,0:T(8,128)(2,1)} async-done(((bf16[1024,1024]{1,0:T(8,128)(2,1)}), bf16[128,1024]{1,0:T(8,128)(2,1)}) %reduce-scatter.72.cloned.1.call-update) | async-done | bytes 262160
  703.6 68.8 %reduce-scatter.70.cloned.1.call-done = bf16[128,1024]{1,0:T(8,128)(2,1)} async-done(((bf16[1024,1024]{1,0:T(8,128)(2,1)}), bf16[128,1024]{1,0:T(8,128)(2,1)}) %reduce-scatter.70.cloned.1.call-update) | async-done | bytes 262160
  774.5 149.4 %reduce-scatter.68.cloned.1.call-done = bf16[512,1024]{1,0:T(8,128)(2,1)} async-done(((bf16[4096,1024]{1,0:T(8,128)(2,1)}), bf16[512,1024]{1,0:T(8,128)(2,1)}) %reduce-scatter.68.cloned.1.call-update) | async-done | bytes 1048592 | tf_op jit(solution)/shard_map/reduce_scatter | solution.py:298
  923.9 2.8 convert_element_type.355
  926.7 149.4 %reduce-scatter.78.cloned.1.call-done = bf16[128,4096]{1,0:T(8,128)(2,1)} async-done(((bf16[1024,4096]{1,0:T(8,128)(2,1)}), bf16[128,4096]{1,0:T(8,128)(2,1)}) %reduce-scatter.78.cloned.1.call-update) | async-done | bytes 1048592
  1079.3 148.5 %reduce-scatter.76.cloned.1.call-done = bf16[128,4096]{1,0:T(8,128)(2,1)} async-done(((bf16[1024,4096]{1,0:T(8,128)(2,1)}), bf16[128,4096]{1,0:T(8,128)(2,1)}) %reduce-scatter.76.cloned.1.call-update) | async-done | bytes 1048592
  (374 shorter events, 156.0 us)
Async XLA Ops:
  7.2 81.8 %copy-start = (bf16[1024,1024]{1,0:T(8,128)(2,1)S(1)}, bf16[1024,1024]{1,0:T(8,128)(2,1)}, u32[]{:S(2)}) copy-start(bf16[1024,1024]{1,0:T(8,128)(2,1)} %param.22) | copy-start | bytes 6291460
  11.4 21.7 %all-to-all-start = ((bf16[2,8,32,512]{3,2,0,1:T(8,128)(2,1)}), bf16[2,8,32,512]{3,2,0,1:T(8,128)(2,1)S(1)}, u32[]{:S(2)}, u32[]{:S(2)}) async-start(bf16[2,8,32,512]{3,2,0,1:T(8,128)(2,1)} %copy.151), calls=%async_computation | async-start | bytes 1048576 | tf_op jit(solution)/shard_map/all_to_all | solution.py:148
  18.6 60.1 %reduce-scatter.42.cloned.1.call-start = ((), (), s32[]{:S(2)}) async-start(), calls=%async_computation.31 | async-start | bytes 4718592 | tf_op jit(solution)/shard_map/reduce_scatter | solution.py:100
  26.6 14.8 %copy-start.63 = (f32[512]{0:T(512)S(1)}, f32[512]{0:T(512)}, u32[]{:S(2)}) copy-start(f32[512]{0:T(512)} %param.18) | copy-start | bytes 6148
  40.8 8.7 copy-start.73
  40.9 8.7 copy-start.75
  56.7 24.7 %reduce-scatter.34.cloned.1.call-start = ((), (), s32[]{:S(2)}) async-start(), calls=%async_computation.26 | async-start | bytes 4718592 | tf_op jit(solution)/shard_map/reduce_scatter | solution.py:100
  71.3 72.7 %reduce-scatter.36.cloned.1.call-start = ((), (), s32[]{:S(2)}) async-start(), calls=%async_computation.27 | async-start | bytes 786432 | tf_op jit(solution)/shard_map/reduce_scatter | solution.py:108
  76.4 22.6 %copy-start.69 = (f32[256]{0:T(256)}, f32[256]{0:T(256)S(1)}, u32[]{:S(2)}) copy-start(f32[256]{0:T(256)S(1)} %get-tuple-element.160) | copy-start | bytes 3076
  76.5 22.6 %copy-start.71 = (f32[256]{0:T(256)}, f32[256]{0:T(256)S(1)}, u32[]{:S(2)}) copy-start(f32[256]{0:T(256)S(1)} %get-tuple-element.161) | copy-start | bytes 3076
  83.7 6.9 copy-start.42
  90.5 53.5 %reduce-scatter.44.cloned.1.call-start = ((), (), s32[]{:S(2)}) async-start(), calls=%async_computation.32 | async-start | bytes 786432 | tf_op jit(solution)/shard_map/reduce_scatter | solution.py:108
  99.0 116.4 %reduce-scatter.58.cloned.1.call-start = ((), (), s32[]{:S(2)}) async-start(), calls=%async_computation.42 | async-start | bytes 6291456 | tf_op jit(solution)/shard_map/reduce_scatter | solution.py:100
  119.7 95.7 %reduce-scatter.46.cloned.1.call-start = ((), (), s32[]{:S(2)}) async-start(), calls=%async_computation.33 | async-start | bytes 12582912 | tf_op jit(solution)/shard_map/reduce_scatter | solution.py:100
  131.7 24.2 %copy-start.59 = (f32[512]{0:T(512)S(1)}, f32[512]{0:T(512)}, u32[]{:S(2)}) copy-start(f32[512]{0:T(512)} %param.23) | copy-start | bytes 6148
  155.9 9.8 copy-start.65
  176.8 45.1 %reduce-scatter.50.cloned.1.call-start = ((), (), s32[]{:S(2)}) async-start(), calls=%async_computation.36 | async-start | bytes 6291456 | tf_op jit(solution)/shard_map/reduce_scatter | solution.py:100
  194.4 37.6 %reduce-scatter.38.cloned.1.call-start = ((), (), s32[]{:S(2)}) async-start(), calls=%async_computation.28 | async-start | bytes 12582912 | tf_op jit(solution)/shard_map/reduce_scatter | solution.py:100
  214.9 33.6 %all-gather.15.cloned.1.call-start = ((), (), s32[]{:S(2)}) async-start(), calls=%async_computation.43 | async-start | bytes 6291456 | tf_op jit(solution)/shard_map/all_gather | solution.py:104
  221.9 42.9 %all-gather.11.cloned.1.call-start = ((), (), s32[]{:S(2)}) async-start(), calls=%async_computation.37 | async-start | bytes 6291456 | tf_op jit(solution)/shard_map/all_gather | solution.py:104
  238.4 39.6 %all-gather.9.cloned.1.call-start = ((), (), s32[]{:S(2)}) async-start(), calls=%async_computation.34 | async-start | bytes 3145728 | tf_op jit(solution)/shard_map/all_gather | solution.py:104
  239.2 57.3 %reduce-scatter.60.cloned.1.call-start = ((), (), s32[]{:S(2)}) async-start(), calls=%async_computation.44 | async-start | bytes 786432 | tf_op jit(solution)/shard_map/reduce_scatter | solution.py:108
  258.6 55.4 %reduce-scatter.52.cloned.1.call-start = ((), (), s32[]{:S(2)}) async-start(), calls=%async_computation.38 | async-start | bytes 786432 | tf_op jit(solution)/shard_map/reduce_scatter | solution.py:108
  274.9 39.1 %copy-start.10 = (bf16[256,512]{1,0:T(8,128)(2,1)S(1)}, bf16[256,512]{1,0:T(8,128)(2,1)}, u32[]{:S(2)}) copy-start(bf16[256,512]{1,0:T(8,128)(2,1)} %reduce-scatter.44.cloned.1.call-done) | copy-start | bytes 786436
  274.9 56.3 %reduce-scatter.48.cloned.1.call-start = ((), (), s32[]{:S(2)}) async-start(), calls=%async_computation.35 | async-start | bytes 786432 | tf_op jit(solution)/shard_map/reduce_scatter | solution.py:108
  285.2 72.9 %reduce-scatter.54.cloned.1.call-start = ((), (), s32[]{:S(2)}) async-start(), calls=%async_computation.39 | async-start | bytes 1572864 | tf_op jit(solution)/shard_map/reduce_scatter | solution.py:100
  345.1 22.8 %reduce-scatter.62.cloned.1.call-start = ((), (), s32[]{:S(2)}) async-start(), calls=%async_computation.45 | async-start | bytes 1572864 | tf_op jit(solution)/shard_map/reduce_scatter | solution.py:100
  355.8 45.5 %all-gather.13.cloned.1.call-start = ((), (), s32[]{:S(2)}) async-start(), calls=%async_computation.40 | async-start | bytes 2359296 | tf_op jit(solution)/shard_map/all_gather | solution.py:104
  388.9 22.4 %all-gather.17.cloned.1.call-start = ((), (), s32[]{:S(2)}) async-start(), calls=%async_computation.46 | async-start | bytes 2359296 | tf_op jit(solution)/shard_map/all_gather | solution.py:104
  400.5 24.3 %all-gather.7.cloned.1.call-start = ((), (), s32[]{:S(2)}) async-start(), calls=%async_computation.29 | async-start | bytes 3145728 | tf_op jit(solution)/shard_map/all_gather | solution.py:104
  401.2 147.3 %reduce-scatter.56.cloned.1.call-start = ((), (), s32[]{:S(2)}) async-start(), calls=%async_computation.41 | async-start | bytes 786432 | tf_op jit(solution)/shard_map/reduce_scatter | solution.py:108
  406.6 142.0 %reduce-scatter.64.cloned.1.call-start = ((), (), s32[]{:S(2)}) async-start(), calls=%async_computation.47 | async-start | bytes 786432 | tf_op jit(solution)/shard_map/reduce_scatter | solution.py:108
  416.7 15.6 %copy-start.21 = (bf16[256,1024]{1,0:T(8,128)(2,1)S(1)}, bf16[256,1024]{1,0:T(8,128)(2,1)}, u32[]{:S(2)}) copy-start(bf16[256,1024]{1,0:T(8,128)(2,1)} %copy-done.20) | copy-start | bytes 1572868
  416.7 141.6 %reduce-scatter.40.cloned.1.call-start = ((), (), s32[]{:S(2)}) async-start(), calls=%async_computation.30 | async-start | bytes 786432 | tf_op jit(solution)/shard_map/reduce_scatter | solution.py:108
  432.0 164.4 %reduce-scatter.66.cloned.1.call-start = ((), (), s32[]{:S(2)}) async-start(), calls=%async_computation.48 | async-start | bytes 2359296 | tf_op jit(solution)/shard_map/reduce_scatter | solution.py:286
  435.3 195.2 %reduce-scatter.74.cloned.1.call-start = ((), (), s32[]{:S(2)}) async-start(), calls=%async_computation.52 | async-start | bytes 2359296
  448.3 253.2 %reduce-scatter.72.cloned.1.call-start = ((), (), s32[]{:S(2)}) async-start(), calls=%async_computation.51 | async-start | bytes 2359296
  452.3 320.1 %reduce-scatter.70.cloned.1.call-start = ((), (), s32[]{:S(2)}) async-start(), calls=%async_computation.50 | async-start | bytes 2359296
  455.0 10.9 copy-start.18
  455.0 468.9 %reduce-scatter.68.cloned.1.call-start = ((), (), s32[]{:S(2)}) async-start(), calls=%async_computation.49 | async-start | bytes 9437184 | tf_op jit(solution)/shard_map/reduce_scatter | solution.py:298
  456.5 9.3 copy-start.9
  477.6 16.8 %copy-start.30 = (bf16[256,1024]{1,0:T(8,128)(2,1)S(1)}, bf16[256,1024]{1,0:T(8,128)(2,1)}, u32[]{:S(2)}) copy-start(bf16[256,1024]{1,0:T(8,128)(2,1)} %copy-done.29) | copy-start | bytes 1572868
  477.6 598.5 %reduce-scatter.78.cloned.1.call-start = ((), (), s32[]{:S(2)}) async-start(), calls=%async_computation.54 | async-start | bytes 9437184
  478.6 15.7 %copy-start.23 = (bf16[2,256,4096]{1,2,0:T(8,128)(2,1)S(1)}, bf16[2,256,4096]{1,2,0:T(8,128)(2,1)}, u32[]{:S(2)}) copy-start(bf16[2,256,4096]{1,2,0:T(8,128)(2,1)} %all-gather.15.cloned.1.call-done) | copy-start | bytes 12582916
  536.6 691.2 %reduce-scatter.76.cloned.1.call-start = ((), (), s32[]{:S(2)}) async-start(), calls=%async_computation.53 | async-start | bytes 9437184
  548.5 9.8 copy-start.84
  548.5 9.8 copy-start.11
  548.5 9.8 copy-start.22
  548.5 9.8 copy-start.26
  548.5 9.8 copy-start.70
  548.5 9.8 copy-start.77
  548.5 11.4 copy-start.39
  559.8 7.4 copy-start.68
  559.9 8.2 copy-start.82
  559.9 8.2 copy-start.25
  559.9 8.2 copy-start.41
  559.9 8.2 copy-start.66
  559.9 8.2 copy-start.72
  559.9 8.2 copy-start.78
  561.3 30.1 %all-to-all-start.1 = ((bf16[2,1,256,512]{3,0,1,2:T(2,128)(2,1)}), bf16[2,1,256,512]{3,0,1,2:T(2,128)(2,1)S(1)}, u32[]{:S(2)}, u32[]{:S(2)}) async-start(bf16[2,1,256,512]{3,0,1,2:T(2,128)(2,1)} %copy.161), calls=%async_computation.9 | async-start | bytes 1048576 | tf_op jit(solution)/shard_map/all_to_all | solution.py:303
  568.1 27.0 %copy-start.85 = (u32[32]{0:T(128)S(1)}, u32[32]{0:T(128)}, u32[]{:S(2)}) copy-start(u32[32]{0:T(128)} %constant.126) | copy-start | bytes 388
  568.1 28.3 %copy-start.79 = (f32[512]{0:T(512)S(1)}, f32[512]{0:T(512)}, u32[]{:S(2)}) copy-start(f32[512]{0:T(512)} %get-tuple-element.60) | copy-start | bytes 6148
  568.1 28.3 %copy-start.80 = (f32[512]{0:T(512)S(1)}, f32[512]{0:T(512)}, u32[]{:S(2)}) copy-start(f32[512]{0:T(512)} %get-tuple-element.69) | copy-start | bytes 6148
  591.4 30.8 %all-to-all-start.2 = ((bf16[2,1,256,512]{3,0,1,2:T(2,128)(2,1)}), bf16[2,1,256,512]{3,0,1,2:T(2,128)(2,1)S(1)}, u32[]{:S(2)}, u32[]{:S(2)}) async-start(bf16[2,1,256,512]{3,0,1,2:T(2,128)(2,1)} %copy.185), calls=%async_computation.18 | async-start | bytes 1048576 | tf_op jit(solution)/shard_map/all_to_all | solution.py:306
  (54 other events, 89.2 us)
Sparse Core Ops, SparseCore 0:
  56.8 9.9 reduce-scatter.41
  71.4 9.8 reduce-scatter.33
  90.7 17.1 reduce-scatter.35
  110.6 14.2 reduce-scatter.43
  127.1 12.0 reduce-scatter.57
  176.9 16.6 reduce-scatter.45
  195.9 13.2 reduce-scatter.49
  215.0 16.9 reduce-scatter.37
  233.5 14.8 all-gather.14
  249.8 14.8 all-gather.10
  266.3 11.7 all-gather.8
  280.7 15.7 reduce-scatter.59
  299.4 14.5 reduce-scatter.51
  316.6 14.5 reduce-scatter.47
  345.2 8.5 reduce-scatter.53
  355.9 9.6 reduce-scatter.61
  389.1 9.7 all-gather.12
  400.6 10.7 all-gather.16
  413.0 11.7 all-gather.6
  427.5 15.7 reduce-scatter.55
  446.1 14.5 reduce-scatter.63
  463.6 14.5 reduce-scatter.39
  481.7 67.7 reduce-scatter.65
  552.9 77.5 reduce-scatter.73
  634.6 66.8 reduce-scatter.71
  705.5 66.8 reduce-scatter.69
  775.9 147.9 reduce-scatter.67
  927.9 148.0 reduce-scatter.77
  1079.7 148.0 reduce-scatter.75
